TPU v7x, 128 devices: a whole 4x4x4 slice. The times are simulated.
128 devices in a mesh: state: 4 (over y_lo, core), domain: 32 (over z, y_hi, x).
Axes of the slice: x: 4, y: 4 (y_hi: 2, y_lo: 2; y = y_hi * 2 + y_lo), z: 4, core: 2. Of those that a mesh axis runs over, the one named last changes fastest.
Arguments:
- orbitals: float32 [2, 4, 224, 25600], P(None, 'state', 'domain'), may hold values from -6 to 6
- occupation: float32 [4], P('state'), may hold values from 8e-07 to 3.2e-06
- potential: float32 [224, 25600], P('domain'), may hold values from 0 to 2
- background: float32 [224, 25600], P('domain'), may hold values from 0.005 to 270, as said below
- layer_start: int32 [33], replicated, may hold values from 0 to 160, as said below
Outputs:
- orbitals_next: float32 [2, 4, 224, 25600], P(None, 'state', 'domain')
- potential_next: float32 [224, 25600], P('domain')
Inputs may be any that keep to these rules, and one draw needn't show every extreme that they name: layer_start[d] - 5 d lies in 0..2, is 0 for the first and the last entry and 2 for the last domain's start, so each domain owns 3 to 7 layers and some domain owns exactly 7. `background`: positive.
All inputs are finite; a program needn't handle non-finite values.
Results may differ from a plain program's by a relative error of at most 0.000071.
Values sent between devices are 32-bit elements; how exact they have to be, the bound alone decides.
A program may use at most 128 MiB of HBM per device.

v0:
```python
import functools
import math

import jax
import jax.numpy as jnp
import numpy as np
from jax import lax
from jax.experimental import pallas as pl
from jax.experimental.pallas import tpu as pltpu
from jax.sharding import PartitionSpec as P

SIDE = 160
SLAB = 5
TERMS = 4
LAYERS = 7
PLANE = SIDE * SIDE
GROUPS = 40
LANES = 640
CHUNKS = 5
CHUNK_GROUPS = 8
OWNERS = 100
PAIRS = 50
DOMAINS = 32
STATES = 4
CHIPS = 64

time_step = 0.3
four_pi = 4.0 * math.pi
two_pi = 2.0 * math.pi
MESH = pl.DeviceIdType.MESH
f32 = jnp.float32
i32 = jnp.int32
bf16 = jnp.bfloat16


def halves(table):
    table = np.asarray(table, np.float32)
    high = table.astype(bf16)
    low = (table - high.astype(np.float32)).astype(bf16)
    return np.stack([high, low])


def real_basis():
    n = SIDE
    j = np.arange(n)
    rows = []
    for i in range(n):
        if i == 0:
            rows.append(np.full(n, math.sqrt(1.0 / n)))
        elif i < n // 2:
            rows.append(math.sqrt(2.0 / n) * np.cos(2 * np.pi * ((i * j) % n) / n))
        elif i == n // 2:
            rows.append(math.sqrt(1.0 / n) * np.where(j % 2 == 0, 1.0, -1.0))
        else:
            m = i - n // 2
            rows.append(math.sqrt(2.0 / n) * np.sin(2 * np.pi * ((m * j) % n) / n))
    return np.stack(rows)


def tables():
    q = real_basis()
    forward_z = np.zeros((4, 256, 256))
    inverse_z = np.zeros((4, 256, 256))
    for r in range(4):
        forward_z[r, 32 * r : 32 * r + SIDE, :SIDE] = q.T
        inverse_z[r, :SIDE, 32 * r : 32 * r + SIDE] = q
    order = np.array([4 * g + r for r in range(4) for g in range(GROUPS)])
    forward_y = q[:, order]
    inverse_y = forward_y.T
    x_table = np.zeros((SIDE, 256))
    x_table[:, :SIDE] = q
    x_back = np.zeros((256, SIDE))
    x_back[:SIDE, :] = q.T
    return [halves(t) for t in (forward_z, forward_y, inverse_y, inverse_z, x_table, x_back)]


def split(value):
    high = value.astype(bf16)
    low = (value - high.astype(f32)).astype(bf16)
    return high, low


def dot(a, b):
    return jnp.dot(a, b, preferred_element_type=f32)


def dot3(a, b):
    return dot(a[0], b[0]) + (dot(a[0], b[1]) + dot(a[1], b[0]))


def kernel(
    starts, occ, orb_hbm, pot_hbm, bg_hbm, fz_hbm, fy_hbm, iy_hbm, iz_hbm, xt_hbm, xb_hbm,
    psi_out, field_out,
    raw, pot, bg, fz, fy, iy, iz, xt, xb,
    cur, psi, diag, half, ion,
    send_lo, send_hi, halo_lo, halo_hi,
    rho_own, rho_rx, rho_chip, rho_y, xc,
    za, zb, e_rho, e_ion, recv_rho, recv_ion, result, spec, hsc, field,
    load_sem, table_sem, out_sem,
    send_lo_sem, send_hi_sem, recv_lo_sem, recv_hi_sem,
    part_send, part_recv, y_send, y_recv, xc_send, xc_recv,
    fwd_send, rho_recv, ion_send, ion_recv, back_send, back_recv, mid_send, mid_recv,
    ready_a, ready_b,
):
    s = lax.axis_index("state")
    d = lax.axis_index("domain")
    core = s % 2
    ylo = s // 2
    chip = d * 2 + ylo

    def dev(state, domain):
        return {"state": state, "domain": domain}

    partner = dev(ylo * 2 + 1 - core, d)
    across = dev((1 - ylo) * 2 + core, d)
    has_low = d > 0
    has_high = d < DOMAINS - 1
    low_dev = dev(s, jnp.maximum(d - 1, 0))
    high_dev = dev(s, jnp.minimum(d + 1, DOMAINS - 1))
    octet = d // 8
    place = d % 8

    barrier = pltpu.get_barrier_semaphore()

    def greet(state, domain):
        pl.semaphore_signal(barrier, inc=1, device_id=dev(state, domain), device_id_type=MESH)

    for step in range(1, 8):
        greet(s, octet * 8 + (place + step) % 8)
    for step in range(1, 4):
        greet((s + step) % 4, d)
        greet(s, (d + 8 * step) % DOMAINS)
    cross_low = jnp.logical_and(place == 0, has_low)
    cross_high = jnp.logical_and(place == 7, has_high)

    @pl.when(cross_low)
    def _():
        greet(s, jnp.maximum(d - 1, 0))

    @pl.when(cross_high)
    def _():
        greet(s, jnp.minimum(d + 1, DOMAINS - 1))

    def loads(ch):
        lanes = pl.ds(ch * (CHUNK_GROUPS * LANES), CHUNK_GROUPS * LANES)
        return (
            pltpu.make_async_copy(orb_hbm.at[:, :, lanes], raw.at[:, :, lanes], load_sem.at[0, ch]),
            pltpu.make_async_copy(pot_hbm.at[:, lanes], pot.at[:, lanes], load_sem.at[1, ch]),
            pltpu.make_async_copy(bg_hbm.at[:, lanes], bg.at[:, lanes], load_sem.at[2, ch]),
        )

    for ch in range(CHUNKS):
        for copy in loads(ch):
            copy.start()
    table_copies = [
        pltpu.make_async_copy(src, dst, table_sem.at[i])
        for i, (src, dst) in enumerate(
            ((fz_hbm, fz), (fy_hbm, fy), (iy_hbm, iy), (iz_hbm, iz), (xt_hbm, xt), (xb_hbm, xb))
        )
    ]
    for copy in table_copies:
        copy.start()

    own_start = starts[d]
    thickness = starts[d + 1] - own_start
    top_row = jnp.clip(thickness - 1, 0, LAYERS - 1)
    lane = lax.broadcasted_iota(i32, (8, LANES), 1)
    sub = lax.broadcasted_iota(i32, (8, LANES), 0)
    y_low = (
        (lane >= SIDE).astype(i32) + (lane >= 2 * SIDE).astype(i32) + (lane >= 3 * SIDE).astype(i32)
    )
    z_off = (2 * (lane - SIDE * y_low) - (SIDE - 1)).astype(f32)
    z_square = z_off * z_off
    y_base = (2 * y_low - (SIDE - 1)).astype(f32)
    x_off = (2 * (own_start + sub) - (SIDE - 1)).astype(f32)
    xz_square = jnp.where(sub < thickness, x_off * x_off, 1.0e9) + z_square
    radius = float((SIDE - 2) ** 2)
    is_low = sub == 0
    is_high = sub == top_row

    def mask_of(g):
        y_off = y_base + (8 * g).astype(f32)
        return jnp.where(y_off * y_off + xz_square <= radius, 1.0, 0.0)

    def lanes_of(g):
        return pl.ds(pl.multiple_of(g * LANES, 128), LANES)

    def edge_sends(k, ch):
        to_low = pltpu.make_async_remote_copy(
            send_lo.at[k, ch], halo_hi.at[k, ch], send_lo_sem.at[k, ch], recv_hi_sem.at[k, ch],
            device_id=low_dev, device_id_type=MESH,
        )
        to_high = pltpu.make_async_remote_copy(
            send_hi.at[k, ch], halo_lo.at[k, ch], send_hi_sem.at[k, ch], recv_lo_sem.at[k, ch],
            device_id=high_dev, device_id_type=MESH,
        )
        return to_low, to_high

    def start_edges(k, ch):
        to_low, to_high = edge_sends(k, ch)

        @pl.when(has_low)
        def _():
            to_low.start()

        @pl.when(has_high)
        def _():
            to_high.start()

    def await_edges(k, ch):
        to_low, to_high = edge_sends(k, ch)

        @pl.when(has_low)
        def _():
            to_high.wait_recv()

        @pl.when(has_high)
        def _():
            to_low.wait_recv()

    zero_group = jnp.zeros((8, LANES), f32)
    for which in range(2):
        for c in range(2):
            cur[which, c, 0] = zero_group
            cur[which, c, GROUPS + 1] = zero_group

    @pl.when(jnp.logical_not(has_low))
    def _():
        halo_lo[...] = jnp.zeros(halo_lo.shape, f32)

    @pl.when(jnp.logical_not(has_high))
    def _():
        halo_hi[...] = jnp.zeros(halo_hi.shape, f32)

    pl.semaphore_wait(
        barrier, 13 + jnp.where(cross_low, 1, 0) + jnp.where(cross_high, 1, 0)
    )

    for ch in range(CHUNKS):
        copies = loads(ch)
        copies[0].wait()
        copies[1].wait()

        def first(gi, carry, ch=ch):
            g = ch * CHUNK_GROUPS + gi
            mask = mask_of(g)
            lanes = lanes_of(g)
            diag[g] = zero_group
            half[g] = 0.5 * mask
            diag[g, 0:7, :] = (3.0 + pot[:, lanes]) * mask[0:7, :]
            for c in range(2):
                value = raw[c, :, lanes] * mask[0:7, :]
                cur[0, c, g + 1] = zero_group
                cur[0, c, g + 1, 0:7, :] = value
                psi[c, g] = zero_group
                psi[c, g, 0:7, :] = value
                send_lo[0, ch, c, pl.ds(gi, 1), :] = value[0:1, :]
                send_hi[0, ch, c, pl.ds(gi, 1), :] = cur[0, c, g + 1, pl.ds(top_row, 1), :]
            return carry

        lax.fori_loop(0, CHUNK_GROUPS, first, 0)
        start_edges(0, ch)

    for step in range(1, 4):
        pl.semaphore_signal(ready_a, inc=1, device_id=dev((s + step) % 4, d), device_id_type=MESH)

    def beside(src, c, g, k, ch, gi):
        own = cur[src, c, g + 1]
        before = cur[src, c, g, :, 384:640]
        after = cur[src, c, g + 2, :, 0:256]
        wide = jnp.concatenate([before, own, after], axis=1)
        total = 1152
        shifted = (
            pltpu.roll(wide, 1, 1)
            + pltpu.roll(wide, total - 1, 1)
            + pltpu.roll(wide, SIDE, 1)
            + pltpu.roll(wide, total - SIDE, 1)
        )[:, 256:896]
        low = jnp.broadcast_to(halo_lo[k, ch, c, pl.ds(gi, 1), :], (8, LANES))
        high = jnp.broadcast_to(halo_hi[k, ch, c, pl.ds(gi, 1), :], (8, LANES))
        rim = jnp.where(is_low, low, jnp.where(is_high, high, 0.0))
        stacked = pltpu.roll(own, 1, 0) + pltpu.roll(own, 7, 0)
        return own, shifted + (stacked + rim)

    def taylor(k):
        factor = time_step / k
        src, dst = (k - 1) % 2, k % 2

        def chunk(ch, carry):
            await_edges(k - 1, ch)

            def group(gi, inner):
                g = ch * CHUNK_GROUPS + gi
                diagonal = diag[g]
                weight = half[g]
                applied = []
                for c in range(2):
                    own, around = beside(src, c, g, k - 1, ch, gi)
                    applied.append(diagonal * own - weight * around)
                fresh = (factor * applied[1], -factor * applied[0])
                if k < TERMS:
                    for c in range(2):
                        cur[dst, c, g + 1] = fresh[c]
                        psi[c, g] = psi[c, g] + fresh[c]
                        send_lo[k, ch, c, pl.ds(gi, 1), :] = fresh[c][0:1, :]
                        send_hi[k, ch, c, pl.ds(gi, 1), :] = cur[
                            dst, c, g + 1, pl.ds(top_row, 1), :
                        ]
                else:
                    lanes = lanes_of(g)
                    squares = zero_group
                    for c in range(2):
                        value = psi[c, g] + fresh[c]
                        field_psi = value[0:7, :]
                        raw[c, :, lanes] = field_psi
                        squares = squares + value * value
                    rho_own[g] = occ[0] * squares
                return inner

            lax.fori_loop(0, CHUNK_GROUPS, group, 0)
            if k < TERMS:
                start_edges(k, ch)
            else:
                share_rho(ch).start()
            return carry

        lax.fori_loop(0, CHUNKS, chunk, 0)

    def share_rho(ch):
        rows = pl.ds(ch * CHUNK_GROUPS, CHUNK_GROUPS)
        return pltpu.make_async_remote_copy(
            rho_own.at[rows], rho_rx.at[rows], part_send.at[ch], part_recv.at[ch],
            device_id=partner, device_id_type=MESH,
        )

    def forward_z(src):
        for r in range(4):
            left = src[:, :, 128 * r : 128 * r + 256].reshape(GROUPS * 8, 256)
            out = dot3(split(left), (fz[0, r], fz[1, r]))
            za[r * 320 : (r + 1) * 320, :] = out[:, 0:128]
            zb[r * 320 : (r + 1) * 320, :] = out[:, 128:256]

    def forward_y(dst, slots):
        for slot in slots:
            rows = pl.ds(slot, SIDE, stride=8)
            right = jnp.concatenate([za[rows, :], zb[rows, :]], axis=1)
            out = dot3((fy[0], fy[1]), split(right))
            dst[rows, :] = out[:, 0:128]
            tail = out[:, 128:256]
            packed = tail[0:40, :]
            for j in range(1, 4):
                packed = packed + pltpu.roll(tail[40 * j : 40 * j + 40, :], 32 * j, 1)
            dst[pl.ds(SIDE * 8 + slot, 40, stride=8), :] = packed

    def put_total(dst, partial):
        total = jnp.broadcast_to(jnp.sum(partial, axis=0, keepdims=True), (200, 128))
        dst[pl.ds(7, 200, stride=8), :] = total

    def fold(value):
        part = value[:, 0:128]
        for j in range(1, 5):
            part = part + value[:, 128 * j : 128 * j + 128]
        return part

    taylor(1)

    for ch in range(CHUNKS):
        loads(ch)[2].wait()

    def ion_group(g, acc):
        ion[g] = zero_group
        value = bg[:, lanes_of(g)] * (2.0 * half[g, 0:7, :])
        ion[g, 0:7, :] = value
        return acc + fold(ion[g])

    ion_total = lax.fori_loop(0, GROUPS, ion_group, jnp.zeros((8, 128), f32))
    for copy in table_copies:
        copy.wait()
    forward_z(ion)

    taylor(2)
    forward_y(e_ion, range(0, 4))

    pl.semaphore_wait(ready_a, 3)
    for step in range(1, 4):
        pl.semaphore_signal(
            ready_b, inc=1, device_id=dev(s, (d + 8 * step) % DOMAINS), device_id_type=MESH
        )

    taylor(3)
    forward_y(e_ion, range(4, 7))
    put_total(e_ion, ion_total)
    pl.semaphore_wait(ready_b, 3)

    other = 1 - core

    def owner_dev(p):
        place_of = (p * 32) // 25
        return dev((place_of % 2) * 2 + other, place_of // 2)

    def column_rows(p, half_of):
        return pl.ds(pl.multiple_of((2 * p + half_of) * 16, 16), 16)

    def send_ion(j):
        p = 2 * ((j + d) % 25) + ylo
        return pltpu.make_async_remote_copy(
            e_ion.at[column_rows(p, other), :],
            recv_ion.at[pl.ds(pl.multiple_of(d * 16, 16), 16), :],
            ion_send, ion_recv, device_id=owner_dev(p), device_id_type=MESH,
        )

    def send_rho(j):
        p = (j + (chip * 25) // 32) % PAIRS
        return pltpu.make_async_remote_copy(
            e_rho.at[column_rows(p, other), :],
            recv_rho.at[pl.ds(pl.multiple_of((ylo * DOMAINS + d) * 16, 16), 16), :],
            fwd_send, rho_recv, device_id=owner_dev(p), device_id_type=MESH,
        )

    def start_all(make, count):
        def one(j, carry):
            make(j).start()
            return carry

        lax.fori_loop(0, count, one, 0)

    start_all(send_ion, 25)

    taylor(4)
    psi_copy = pltpu.make_async_copy(raw, psi_out, out_sem.at[0])
    psi_copy.start()

    def chip_sum(ch, acc):
        share_rho(ch).wait_recv()

        def group(gi, inner):
            g = ch * CHUNK_GROUPS + gi
            value = rho_own[g] + rho_rx[g]
            rho_chip[g] = value
            return inner + fold(value)

        return lax.fori_loop(0, CHUNK_GROUPS, group, acc)

    rho_total = lax.fori_loop(0, CHUNKS, chip_sum, jnp.zeros((8, 128), f32))

    forward_z(rho_chip)
    forward_y(e_rho, range(7))
    put_total(e_rho, rho_total)
    start_all(send_rho, PAIRS)

    half_rows = pl.ds(pl.multiple_of(core * 20, 4), 20)
    y_copy = pltpu.make_async_remote_copy(
        rho_chip.at[half_rows], rho_y, y_send, y_recv, device_id=across, device_id_type=MESH
    )
    y_copy.start()

    pair_of = (chip * 25 + 31) // 32
    is_owner = jnp.logical_and((pair_of * 32) // 25 == chip, pair_of < PAIRS)

    def await_bytes(ref, sem):
        pltpu.make_async_copy(ref, ref, sem).wait()

    def send_back(j):
        q = (j + chip) % CHIPS
        return pltpu.make_async_remote_copy(
            result.at[pl.ds(pl.multiple_of((q // 2) * 16, 16), 16), :],
            spec.at[pl.ds(pl.multiple_of((2 * pair_of + core) * 16, 16), 16), :],
            back_send, back_recv,
            device_id=dev((q % 2) * 2 + other, q // 2), device_id_type=MESH,
        )

    @pl.when(is_owner)
    def _():
        lane256 = lax.broadcasted_iota(i32, (SIDE, 256), 1)
        row160 = lax.broadcasted_iota(i32, (SIDE, 256), 0)
        lane_row = lax.broadcasted_iota(i32, (8, 256), 1)
        slot_row = lane_row % 8
        dom_row = lane_row // 8
        where_x = jnp.full((8, 256), -1, i32)
        pieces = []
        sub256 = lax.broadcasted_iota(i32, (8, 256), 0)
        for k in range(DOMAINS):
            first_x = starts[k]
            count = starts[k + 1] - first_x
            where_x = jnp.where(
                jnp.logical_and(dom_row == k, slot_row < count), first_x + slot_row, where_x
            )
            hit = jnp.logical_and(lane_row == first_x + sub256, sub256 < count)
            pieces.append(jnp.where(hit, 1.0, 0.0))
        select_back = jnp.concatenate(pieces, axis=0).astype(bf16)
        wide_x = jnp.broadcast_to(where_x[0:1, :], (256, 256))
        row256 = lax.broadcasted_iota(i32, (256, 256), 0)
        select = jnp.where(wide_x == row256, 1.0, 0.0).astype(bf16)
        x_fwd = (dot(xt[0], select).astype(bf16), dot(xt[1], select).astype(bf16))
        x_inv = (dot(select_back, xb[0]).astype(bf16), dot(select_back, xb[1]).astype(bf16))
        o = 2 * pair_of + core
        unit = 2 * o + lane256 // 128
        low_lane = lane256 % 128
        is_tail = unit >= SIDE
        ky = jnp.where(is_tail, 40 * (low_lane // 32) + unit - SIDE, unit)
        kz = jnp.where(is_tail, 128 + low_lane % 32, low_lane)

        def wave(index):
            folded = jnp.where(2 * index <= SIDE, index, index - SIDE // 2)
            number = folded.astype(f32) * (two_pi / SIDE)
            return number * number

        squared = wave(row160) + wave(ky) + wave(kz)
        coulomb = jnp.where(squared > 0, four_pi / jnp.where(squared > 0, squared, 1.0), 0.0)

        await_bytes(recv_ion, ion_recv)
        await_bytes(recv_rho, rho_recv)
        ions = recv_ion[...].reshape(DOMAINS, 2, 8, 128)
        dens = recv_rho[...].reshape(2, DOMAINS, 2, 8, 128)
        dens = dens[0] + dens[1]
        sub8 = lax.broadcasted_iota(i32, (8, 128), 0)

        def total_of(array):
            rows = jnp.sum(array[:, 0], axis=0)
            return jnp.sum(jnp.where(sub8 == 7, rows, 0.0), axis=(0, 1), keepdims=True)

        scale = total_of(dens) / total_of(ions)
        charge = dens - scale.reshape(1, 1, 1, 1) * ions
        right = jnp.concatenate(
            [charge[:, 0].reshape(256, 128), charge[:, 1].reshape(256, 128)], axis=1
        )
        waves = dot3(x_fwd, split(right)) * coulomb
        back = dot3(x_inv, split(waves))
        result[...] = jnp.stack(
            [back[:, 0:128].reshape(DOMAINS, 8, 128), back[:, 128:256].reshape(DOMAINS, 8, 128)],
            axis=1,
        ).reshape(DOMAINS * 16, 128)
        start_all(send_back, CHIPS)

    y_copy.wait_recv()

    def root(i, carry):
        value = (3.0 / math.pi) * (rho_chip[core * 20 + i] + rho_y[i])
        positive = value > 1.0e-37
        safe = jnp.where(positive, value, 1.0)
        guess = jnp.exp(jnp.log(safe) * (1.0 / 3.0))
        guess = (2.0 * guess + safe / (guess * guess)) * (1.0 / 3.0)
        xc[core * 20 + i] = jnp.where(positive, guess, 0.0)
        return carry

    lax.fori_loop(0, 20, root, 0)
    xc_copy = pltpu.make_async_remote_copy(
        xc.at[half_rows], xc.at[half_rows], xc_send, xc_recv,
        device_id=partner, device_id_type=MESH,
    )
    xc_copy.start()

    await_bytes(spec.at[pl.ds(0, 800), :], back_recv)

    def swap(p):
        rows = column_rows(p, other)
        return pltpu.make_async_remote_copy(
            spec.at[rows, :], spec.at[rows, :], mid_send, mid_recv,
            device_id=partner, device_id_type=MESH,
        )

    start_all(swap, PAIRS)
    await_bytes(spec.at[pl.ds(0, 800), :], mid_recv)

    for slot in range(7):
        rows = pl.ds(slot, SIDE, stride=8)
        main = spec[rows, :]
        tail = spec[pl.ds(SIDE * 8 + slot, 40, stride=8), :]
        parts = [tail] + [pltpu.roll(tail, 128 - 32 * j, 1) for j in range(1, 4)]
        right = jnp.concatenate([main, jnp.concatenate(parts, axis=0)], axis=1)
        out = dot3((iy[0], iy[1]), split(right))
        za[rows, :] = out[:, 0:128]
        zb[rows, :] = out[:, 128:256]
    carried = None
    for r in range(4):
        left = jnp.concatenate(
            [za[r * 320 : (r + 1) * 320, :], zb[r * 320 : (r + 1) * 320, :]], axis=1
        )
        out = dot3(split(left), (iz[0, r], iz[1, r]))
        piece = out[:, 0:128]
        if carried is not None:
            piece = piece + carried
        hsc[:, :, 128 * r : 128 * r + 128] = piece.reshape(GROUPS, 8, 128)
        carried = out[:, 128:256]
    hsc[:, :, 512:640] = carried.reshape(GROUPS, 8, 128)

    xc_copy.wait_recv()

    def finish(g, carry):
        value = (hsc[g] - xc[g]) * (2.0 * half[g])
        value = jnp.where(half[g] > 0.0, value, 0.0)
        field[:, lanes_of(g)] = value[0:7, :]
        return carry

    lax.fori_loop(0, GROUPS, finish, 0)
    field_copy = pltpu.make_async_copy(field, field_out, out_sem.at[1])
    field_copy.start()

    for k in range(TERMS):
        def drain(ch, carry, k=k):
            to_low, to_high = edge_sends(k, ch)

            @pl.when(has_low)
            def _():
                to_low.wait_send()

            @pl.when(has_high)
            def _():
                to_high.wait_send()

            return carry

        lax.fori_loop(0, CHUNKS, drain, 0)

    def drain_rho(ch, carry):
        share_rho(ch).wait_send()
        return carry

    lax.fori_loop(0, CHUNKS, drain_rho, 0)
    y_copy.wait_send()
    xc_copy.wait_send()
    await_bytes(e_ion.at[pl.ds(0, 400), :], ion_send)
    await_bytes(e_rho.at[pl.ds(0, 800), :], fwd_send)
    await_bytes(spec.at[pl.ds(0, 800), :], mid_send)

    @pl.when(is_owner)
    def _():
        await_bytes(recv_rho, back_send)

    psi_copy.wait()
    field_copy.wait()


def step(orbitals, occupation, potential, background, layer_start):
    tabs = [jnp.asarray(t) for t in tables()]
    vmem = lambda *shape: pltpu.VMEM(shape, f32)
    dma = pltpu.SemaphoreType.DMA
    anyspace = pl.BlockSpec(memory_space=pl.ANY)
    smem = pl.BlockSpec(memory_space=pltpu.SMEM)
    wide = CHUNK_GROUPS * LANES
    edge = (TERMS, CHUNKS, 2, CHUNK_GROUPS, LANES)
    cube = (GROUPS, 8, LANES)
    columns = (1600, 128)
    scratch = [
        vmem(2, LAYERS, PLANE), vmem(LAYERS, PLANE), vmem(LAYERS, PLANE),
        *[pltpu.VMEM(t.shape, bf16) for t in tabs],
        vmem(2, 2, GROUPS + 2, 8, LANES), vmem(2, *cube), vmem(*cube), vmem(*cube), vmem(*cube),
        vmem(*edge), vmem(*edge), vmem(*edge), vmem(*edge),
        vmem(*cube), vmem(*cube), vmem(*cube), vmem(20, 8, LANES), vmem(*cube),
        vmem(1280, 128), vmem(1280, 128), vmem(*columns), vmem(*columns),
        vmem(1024, 128), vmem(512, 128), vmem(512, 128), vmem(*columns),
        vmem(*cube), vmem(LAYERS, PLANE),
        dma((3, CHUNKS)), dma((6,)), dma((2,)),
        dma((TERMS, CHUNKS)), dma((TERMS, CHUNKS)), dma((TERMS, CHUNKS)), dma((TERMS, CHUNKS)),
        dma((CHUNKS,)), dma((CHUNKS,)),
        *[dma(()) for _ in range(12)],
        pltpu.SemaphoreType.REGULAR, pltpu.SemaphoreType.REGULAR,
    ]
    psi, field = pl.pallas_call(
        kernel,
        out_shape=(
            jax.ShapeDtypeStruct((2, LAYERS, PLANE), f32),
            jax.ShapeDtypeStruct((LAYERS, PLANE), f32),
        ),
        in_specs=[smem, smem] + [anyspace] * 9,
        out_specs=(anyspace, anyspace),
        scratch_shapes=scratch,
        compiler_params=pltpu.CompilerParams(
            collective_id=0, has_side_effects=True, vmem_limit_bytes=60 * 1024 * 1024
        ),
    )(
        layer_start, occupation, orbitals.reshape(2, LAYERS, PLANE), potential, background, *tabs
    )
    return psi.reshape(2, 1, LAYERS, PLANE), field


def solution(mesh):
    return jax.shard_map(
        step,
        mesh=mesh,
        in_specs=(
            P(None, "state", "domain", None),
            P("state"),
            P("domain", None),
            P("domain", None),
            P(),
        ),
        out_specs=(P(None, "state", "domain", None), P("domain", None)),
        check_vma=False,
    )
```

profile of v0, /device:TPU:1, one launch (start us, length us, event | category | flops | bytes accessed | tf_op | source)
XLA Modules:
  0.0 79.9 jit_solution(18338837766918711781)
XLA Ops:
  1.3 2.1 %copy.18 = f32[2,1,7,25600]{3,0,2,1:T(2,128)S(1)} copy(f32[2,1,7,25600]{3,1,2,0:T(1,128)} %param.11) | data formatting | bytes 2867200 | tf_op args[0]
  3.4 1.7 %copy.15.orb_hbm = f32[2,7,25600]{2,1,0:T(8,128)} copy(f32[2,7,25600]{2,0,1:T(2,128)S(1)} %bitcast.4) | data formatting | bytes 2867200 | tf_op jit(solution)/shard_map/reshape | solution.py:672
  5.1 69.9 %shard_map.122 = (f32[2,7,25600]{2,1,0:T(8,128)}, f32[7,25600]{1,0:T(8,128)}) custom-call(s32[33]{0:T(128)} %starts.1, f32[1]{0:T(128)S(6)} %copy.20.occ, f32[2,7,25600]{2,1,0:T(8,128)} %copy.15.orb_hbm, f32[7,25600]{1,0:T(8,128)} %pot_hbm.1, f32[7,25600]{1,0:T(8,128)} %bg_hbm.1, bf16[2,4,256,256]{3,2,1,0:T(8,128)(2,1)} %constant.12.clone.fz_hbm, ...), custom_call_target="tpu_custom_call" | custom-call | tf_op jit(solution)/shard_map/pallas_call | solution.py:659
  75.0 0.0 copy-start
  75.0 4.1 %copy.16 = f32[2,1,7,25600]{3,1,2,0:T(1,128)} copy(f32[2,1,7,25600]{3,2,0,1:T(8,128)} %bitcast.5) | data formatting | bytes 2867200
  79.0 0.0 copy-done
  79.0 0.9 %copy.21 = f32[7,25600]{1,0:T(8,128)} copy(f32[7,25600]{1,0:T(8,128)S(1)} %copy-done) | data formatting | bytes 1433600
Async XLA Ops:
  75.0 4.1 %copy-start = (f32[7,25600]{1,0:T(8,128)S(1)}, f32[7,25600]{1,0:T(8,128)}, u32[]{:S(2)}) copy-start(f32[7,25600]{1,0:T(8,128)} %get-tuple-element.13) | copy-start | bytes 2150404
where the time goes:
time: 80.1 us; the launch traced here: 79.9 us
  Pallas kernels  69.9 us (87%)
  local copies, waits for them, and re-layouts  8.75 us (11%)
  between operations  1.3 us (2%)
    pallas_call x1, Pallas kernels, step(): pl.pallas_call(kernel, out_shape=(jax.ShapeDtypeStruct((2, LAYERS, PLANE)...  69.9 us
    unnamed x5, local copies, waits for them, and re-layouts  7.07 us
    reshape x1, local copies, waits for them, and re-layouts, step(): orbitals.reshape(2, LAYERS, PLANE)  1.68 us

commit v1 on v0

v1 whole, which is shorter than its diff:
```python
import functools
import math

import jax
import jax.numpy as jnp
import numpy as np
from jax import lax
from jax.experimental import pallas as pl
from jax.experimental.pallas import tpu as pltpu
from jax.sharding import PartitionSpec as P

SIDE = 160
SLAB = 5
TERMS = 4
LAYERS = 7
PLANE = SIDE * SIDE
GROUPS = 40
LANES = 640
CHUNKS = 5
CHUNK_GROUPS = 8
OWNERS = 100
PAIRS = 50
DOMAINS = 32
STATES = 4
CHIPS = 64

time_step = 0.3
four_pi = 4.0 * math.pi
two_pi = 2.0 * math.pi
MESH = pl.DeviceIdType.MESH
f32 = jnp.float32
i32 = jnp.int32
bf16 = jnp.bfloat16


def halves(table):
    table = np.asarray(table, np.float32)
    high = table.astype(bf16)
    low = (table - high.astype(np.float32)).astype(bf16)
    return np.stack([high, low])


def real_basis():
    n = SIDE
    j = np.arange(n)
    rows = []
    for i in range(n):
        if i == 0:
            rows.append(np.full(n, math.sqrt(1.0 / n)))
        elif i < n // 2:
            rows.append(math.sqrt(2.0 / n) * np.cos(2 * np.pi * ((i * j) % n) / n))
        elif i == n // 2:
            rows.append(math.sqrt(1.0 / n) * np.where(j % 2 == 0, 1.0, -1.0))
        else:
            m = i - n // 2
            rows.append(math.sqrt(2.0 / n) * np.sin(2 * np.pi * ((m * j) % n) / n))
    return np.stack(rows)


def tables():
    q = real_basis()
    side_table = np.zeros((SIDE, 256))
    side_table[:, :SIDE] = q.T
    order = np.array([4 * g + r for r in range(4) for g in range(GROUPS)])
    forward_y = q[:, order]
    x_table = np.zeros((SIDE, 256))
    x_table[:, :SIDE] = q
    x_back = np.zeros((256, SIDE))
    x_back[:SIDE, :] = q.T
    half_y = np.zeros((2, 96, SIDE))
    for which in range(2):
        for j in range(4):
            for q in range(20):
                half_y[which, 24 * j + q] = forward_y[40 * j + 4 * (q // 2) + 2 * which + q % 2]
    high, low = halves(half_y)
    left_y = np.concatenate([high, high, low], axis=2)
    high, low = halves(forward_y.T)
    left_back = np.concatenate([high, high, low], axis=1)
    return [halves(side_table), left_y, left_back, halves(x_table), halves(x_back)]


def split(value):
    high = value.astype(bf16)
    low = (value - high.astype(f32)).astype(bf16)
    return high, low


def dot(a, b):
    return jnp.dot(a, b, preferred_element_type=f32)


def dot_t(a, b):
    dims = (((1,), (1,)), ((), ()))
    return lax.dot_general(a, b, dims, preferred_element_type=f32)


def stack_left(value, axis=1):
    high, low = split(value)
    return jnp.concatenate([high, high, low], axis=axis)


def stack_right(value, axis=0):
    high, low = split(value)
    return jnp.concatenate([high, low, high], axis=axis)


def kernel(
    starts, occ, orb_hbm, pot_hbm, bg_hbm, qz_hbm, fy_hbm, iy_hbm, xt_hbm, xb_hbm,
    psi_out, field_out,
    raw, pot, bg, qz, fy, iy, xt, xb, fz,
    cur_a, cur_b, psi, diag, half, ion,
    send_lo, send_hi, halo_lo, halo_hi,
    rho_own, rho_rx, rho_chip, rho_cols, rho_y, xc,
    za, zb, e_rho, e_ion, recv_rho, recv_ion, result, spec, hsc, field,
    x_fwd, x_inv, coulomb,
    load_sem, table_sem, out_sem,
    send_lo_sem, send_hi_sem, recv_lo_sem, recv_hi_sem,
    part_send, part_recv, y_send, y_recv, xc_send, xc_recv,
    fwd_send, rho_recv, ion_send, ion_recv, back_send, back_recv, mid_send, mid_recv,
    ready_a, ready_b,
):
    s = lax.axis_index("state")
    d = lax.axis_index("domain")
    core = s & 1
    ylo = s >> 1
    chip = d * 2 + ylo

    def dev(state, domain):
        return {"state": state, "domain": domain}

    partner = dev(ylo * 2 + 1 - core, d)
    across = dev((1 - ylo) * 2 + core, d)
    has_low = d > 0
    has_high = d < DOMAINS - 1
    low_dev = dev(s, jnp.maximum(d - 1, 0))
    high_dev = dev(s, jnp.minimum(d + 1, DOMAINS - 1))
    octet = d >> 3
    place = d & 7

    barrier = pltpu.get_barrier_semaphore()

    def greet(state, domain):
        pl.semaphore_signal(barrier, inc=1, device_id=dev(state, domain), device_id_type=MESH)

    for step in range(1, 8):
        greet(s, octet * 8 + ((place + step) & 7))
    for step in range(1, 4):
        greet((s + step) & 3, d)
        greet(s, (d + 8 * step) & (DOMAINS - 1))
    cross_low = jnp.logical_and(place == 0, has_low)
    cross_high = jnp.logical_and(place == 7, has_high)

    @pl.when(cross_low)
    def _():
        greet(s, jnp.maximum(d - 1, 0))

    @pl.when(cross_high)
    def _():
        greet(s, jnp.minimum(d + 1, DOMAINS - 1))

    orb_copy = pltpu.make_async_copy(orb_hbm, raw.at[pl.ds(0, 2800), :], load_sem.at[0])
    pot_copy = pltpu.make_async_copy(pot_hbm, pot, load_sem.at[1])
    bg_copy = pltpu.make_async_copy(bg_hbm, bg, load_sem.at[2])
    table_copies = [
        pltpu.make_async_copy(src, dst, table_sem.at[i])
        for i, (src, dst) in enumerate(
            ((qz_hbm, qz), (fy_hbm, fy), (iy_hbm, iy), (xt_hbm, xt), (xb_hbm, xb))
        )
    ]
    for copy in [orb_copy, pot_copy, bg_copy] + table_copies:
        copy.start()

    own_start = starts[d]
    thickness = starts[d + 1] - own_start
    top_row = jnp.clip(thickness - 1, 0, LAYERS - 1)
    lane = lax.broadcasted_iota(i32, (8, 128), 1)
    sub = lax.broadcasted_iota(i32, (8, 128), 0)
    radius = float((SIDE - 2) ** 2)
    x_off = (2 * (own_start + sub) - (SIDE - 1)).astype(f32)
    x_square = jnp.where(sub < thickness, x_off * x_off, 1.0e9)
    yz_parts = []
    for j in range(5):
        flat = lane + 128 * j
        y_low = (
            (flat >= SIDE).astype(i32)
            + (flat >= 2 * SIDE).astype(i32)
            + (flat >= 3 * SIDE).astype(i32)
        )
        z_off = (2 * (flat - SIDE * y_low) - (SIDE - 1)).astype(f32)
        yz_parts.append(((2 * y_low - (SIDE - 1)).astype(f32), x_square + z_off * z_off))
    is_spare = sub == 7
    is_above = sub == top_row + 1
    first_lane = lane == 0
    last_lane = lane == 127
    low_lanes = lane < 32
    high_lanes = lane >= 96

    def inside(g, j):
        y_base, xz_square = yz_parts[j]
        y_off = y_base + (8 * g).astype(f32)
        return y_off * y_off + xz_square <= radius

    def lanes_of(g, j):
        return pl.ds(pl.multiple_of(g * LANES + 128 * j, 128), 128)

    def rows_of(g):
        return pl.ds(pl.multiple_of(g * 8, 8), 8)

    def rows7_of(g):
        return pl.ds(pl.multiple_of(g * 8, 8), 7)

    def edge_sends(k, ch):
        to_low = pltpu.make_async_remote_copy(
            send_lo.at[k, ch], halo_hi.at[k, ch], send_lo_sem.at[k, ch], recv_hi_sem.at[k, ch],
            device_id=low_dev, device_id_type=MESH,
        )
        to_high = pltpu.make_async_remote_copy(
            send_hi.at[k, ch], halo_lo.at[k, ch], send_hi_sem.at[k, ch], recv_lo_sem.at[k, ch],
            device_id=high_dev, device_id_type=MESH,
        )
        return to_low, to_high

    def start_edges(k, ch):
        to_low, to_high = edge_sends(k, ch)

        @pl.when(has_low)
        def _():
            to_low.start()

        @pl.when(has_high)
        def _():
            to_high.start()

    def await_edges(k, ch):
        to_low, to_high = edge_sends(k, ch)

        @pl.when(has_low)
        def _():
            to_high.wait_recv()

        @pl.when(has_high)
        def _():
            to_low.wait_recv()

    zero = jnp.zeros((8, 128), f32)
    for cur in (cur_a, cur_b):
        for c in range(2):
            for j in range(5):
                cur[c, j, 0:8, :] = zero
                cur[c, j, 8 * GROUPS + 8 : 8 * GROUPS + 16, :] = zero

    def pick_edges(cur, k, ch):
        base = (ch * CHUNK_GROUPS + 1) * 8
        for c in range(2):
            for j in range(5):
                view = cur.at[c, j]
                send_lo[k, ch, c, j] = view[pl.ds(base, 8, stride=8), :]
                send_hi[k, ch, c, j] = view[pl.ds(base + top_row, 8, stride=8), :]

    @pl.when(jnp.logical_not(has_low))
    def _():
        halo_lo[...] = jnp.zeros(halo_lo.shape, f32)

    @pl.when(jnp.logical_not(has_high))
    def _():
        halo_hi[...] = jnp.zeros(halo_hi.shape, f32)

    orb_copy.wait()
    pot_copy.wait()

    def first_chunk(ch, carry):
        def first(gi, inner):
            for step_g in range(2):
                g = ch * CHUNK_GROUPS + gi * 2 + step_g
                for j in range(5):
                    keep = inside(g, j)
                    mask = jnp.where(keep, 1.0, 0.0)
                    half[j, rows_of(g), :] = 0.5 * mask
                    diag[j, rows_of(g), :] = zero
                    diag[j, rows7_of(g), :] = (3.0 + pot[:, lanes_of(g, j)]) * mask[0:7, :]
                    for c in range(2):
                        value = raw[pl.ds(c * 1400 + 5 * g + j, 8, stride=200), :]
                        value = jnp.where(keep, value, 0.0)
                        cur_a[c, j, rows_of(g + 1), :] = value
                        psi[c, j, rows_of(g), :] = value
            return inner

        lax.fori_loop(0, CHUNK_GROUPS // 2, first, 0)
        pick_edges(cur_a, 0, ch)
        return carry

    lax.fori_loop(0, CHUNKS, first_chunk, 0)
    pl.semaphore_wait(
        barrier, 13 + jnp.where(cross_low, 1, 0) + jnp.where(cross_high, 1, 0)
    )


    def send_first(ch, carry):
        start_edges(0, ch)
        return carry

    lax.fori_loop(0, CHUNKS, send_first, 0)

    for step in range(1, 4):
        pl.semaphore_signal(ready_a, inc=1, device_id=dev((s + step) & 3, d), device_id_type=MESH)

    span = 4

    def taylor(k):
        factor = time_step / k
        src, dst = (cur_a, cur_b) if k % 2 else (cur_b, cur_a)
        count = 5 * span

        def chunk(ch, carry):
            await_edges(k - 1, ch)

            def block(bi, inner):
                g0 = ch * CHUNK_GROUPS + bi * span

                def tile(c, v):
                    return src[c, v % 5, rows_of(g0 + 1 + v // 5), :]

                applied = []
                for c in range(2):
                    own = {v: tile(c, v) for v in range(-2, count + 2)}
                    right1 = {v: pltpu.roll(own[v], 1, 1) for v in range(-1, count)}
                    left1 = {v: pltpu.roll(own[v], 127, 1) for v in range(0, count + 1)}
                    right32 = {v: pltpu.roll(own[v], 32, 1) for v in range(-2, count - 0)}
                    left32 = {v: pltpu.roll(own[v], 96, 1) for v in range(1, count + 2)}
                    out = []
                    for v in range(count):
                        j, gi = v % 5, bi * span + v // 5
                        near = jnp.where(first_lane, right1[v - 1], right1[v]) + jnp.where(
                            last_lane, left1[v + 1], left1[v]
                        )
                        far = jnp.where(low_lanes, right32[v - 2], right32[v - 1]) + jnp.where(
                            high_lanes, left32[v + 2], left32[v + 1]
                        )
                        low = jnp.broadcast_to(
                            halo_lo[k - 1, ch, c, j, pl.ds(gi, 1), :], (8, 128)
                        )
                        high = jnp.broadcast_to(
                            halo_hi[k - 1, ch, c, j, pl.ds(gi, 1), :], (8, 128)
                        )
                        stacked = pltpu.roll(jnp.where(is_spare, low, own[v]), 1, 0) + pltpu.roll(
                            jnp.where(is_above, high, own[v]), 7, 0
                        )
                        rows = rows_of(g0 + v // 5)
                        out.append(
                            diag[j, rows, :] * own[v]
                            - half[j, rows, :] * ((near + far) + stacked)
                        )
                    applied.append(out)
                for v in range(count):
                    j = v % 5
                    g = g0 + v // 5
                    rows = rows_of(g)
                    fresh = (factor * applied[1][v], -factor * applied[0][v])
                    squares = zero
                    for c in range(2):
                        value = psi[c, j, rows, :] + fresh[c]
                        if k < TERMS:
                            dst[c, j, rows_of(g + 1), :] = fresh[c]
                            psi[c, j, rows, :] = value
                        else:
                            raw[pl.ds(c * 1400 + 5 * g + j, 7, stride=200), :] = value[0:7, :]
                            squares = squares + value * value
                    if k == TERMS:
                        rho_own[g, :, 128 * j : 128 * j + 128] = occ[0] * squares
                return inner

            lax.fori_loop(0, CHUNK_GROUPS // span, block, 0)
            if k < TERMS:
                pick_edges(dst, k, ch)
                start_edges(k, ch)
                return carry
            share_rho(ch).start()
            return chip_sum(ch - 1, ch > 0, carry)

        if k < TERMS:
            return lax.fori_loop(0, CHUNKS, chunk, 0)
        return chip_sum(CHUNKS - 1, None, lax.fori_loop(0, CHUNKS, chunk, zero))

    def chip_sum(ch, live, acc):
        if live is None:
            share_rho(ch).wait_recv()
        else:

            @pl.when(live)
            def _():
                share_rho(ch).wait_recv()

        def group(gi, inner):
            g = ch * CHUNK_GROUPS + gi
            for j in range(5):
                cols = slice(128 * j, 128 * j + 128)
                value = rho_own[g, :, cols] + rho_rx[g, :, cols]
                rho_chip[g, :, cols] = value
                rho_cols[j, rows_of(g), :] = value
                inner = inner + value
            return inner

        count = CHUNK_GROUPS if live is None else jnp.where(live, CHUNK_GROUPS, 0)
        return lax.fori_loop(0, count, group, acc)

    def share_rho(ch):
        rows = pl.ds(ch * CHUNK_GROUPS, CHUNK_GROUPS)
        return pltpu.make_async_remote_copy(
            rho_own.at[rows], rho_rx.at[rows], part_send.at[ch], part_recv.at[ch],
            device_id=partner, device_id_type=MESH,
        )

    def forward_z(src):
        parts = [split(src[j]) for j in range(5)]
        for r in range(4):
            high, low = (
                jnp.concatenate([parts[r][i], parts[r + 1][i]], axis=1) for i in range(2)
            )
            out = dot(jnp.concatenate([high, high, low], axis=1), fz[r])
            za[r * 320 : (r + 1) * 320, :] = out[:, 0:128]
            zb[r * 320 : (r + 1) * 320, :] = out[:, 128:256]

    other = 1 - core

    def forward_y(dst, slots):
        table = fy[other]
        for slot in slots:
            rows = pl.ds(slot, SIDE, stride=8)
            right = jnp.concatenate([za[rows, :], zb[rows, :]], axis=1)
            out = dot(table, stack_right(right))
            dst[pl.ds(slot, 96, stride=8), :] = out[:, 0:128]
            tail = out[:, 128:256]
            packed = tail[0:24, :]
            for j in range(1, 4):
                packed = packed + pltpu.roll(tail[24 * j : 24 * j + 24, :], 32 * j, 1)
            dst[pl.ds(96 * 8 + slot, 24, stride=8), :] = packed

    def put_total(dst, partial):
        total = jnp.broadcast_to(jnp.sum(partial, axis=0, keepdims=True), (120, 128))
        dst[pl.ds(7, 120, stride=8), :] = total

    pair_of = (chip * 25 + 31) >> 5
    is_owner = jnp.logical_and(lax.div(pair_of * 32, 25) == chip, pair_of < PAIRS)

    def build_x_tables():
        @pl.when(is_owner)
        def _():
            lane256 = lax.broadcasted_iota(i32, (SIDE, 256), 1)
            row160 = lax.broadcasted_iota(i32, (SIDE, 256), 0)
            lane_row = lax.broadcasted_iota(i32, (8, 256), 1)
            slot_row = lane_row % 8
            dom_row = lane_row // 8
            where_x = jnp.full((8, 256), -1, i32)
            pieces = []
            sub256 = lax.broadcasted_iota(i32, (8, 256), 0)
            for k in range(DOMAINS):
                first_x = starts[k]
                count = starts[k + 1] - first_x
                where_x = jnp.where(
                    jnp.logical_and(dom_row == k, slot_row < count), first_x + slot_row, where_x
                )
                hit = jnp.logical_and(lane_row == first_x + sub256, sub256 < count)
                pieces.append(jnp.where(hit, 1.0, 0.0))
            select_back = jnp.concatenate(pieces, axis=0).astype(bf16)
            wide_x = jnp.broadcast_to(where_x[0:1, :], (256, 256))
            row256 = lax.broadcasted_iota(i32, (256, 256), 0)
            select = jnp.where(wide_x == row256, 1.0, 0.0).astype(bf16)
            x_high, x_low = (dot(xt[i], select).astype(bf16) for i in range(2))
            x_fwd[...] = jnp.concatenate([x_high, x_high, x_low], axis=1)
            for i in range(2):
                x_inv[i] = dot(select_back, xb[i]).astype(bf16)
            o = 2 * pair_of + core
            unit = 2 * o + lane256 // 128
            low_lane = lane256 % 128
            is_tail = unit >= SIDE
            ky = jnp.where(is_tail, 40 * (low_lane // 32) + unit - SIDE, unit)
            kz = jnp.where(is_tail, 128 + low_lane % 32, low_lane)

            def wave(index):
                folded = jnp.where(2 * index <= SIDE, index, index - SIDE // 2)
                number = folded.astype(f32) * (two_pi / SIDE)
                return number * number

            squared = wave(row160) + wave(ky) + wave(kz)
            coulomb[...] = jnp.where(squared > 0, four_pi / jnp.where(squared > 0, squared, 1.0), 0.0)


    bg_copy.wait()

    def ion_group(g, acc):
        for j in range(5):
            weight = 2.0 * half[j, rows_of(g), :]
            ion[j, rows_of(g), :] = zero
            ion[j, rows7_of(g), :] = bg[:, lanes_of(g, j)] * weight[0:7, :]
            acc = acc + ion[j, rows_of(g), :]
        return acc

    ion_total = lax.fori_loop(0, GROUPS, ion_group, zero)
    for copy in table_copies:
        copy.wait()
    fz[...] = jnp.zeros(fz.shape, bf16)
    for i, which in enumerate((0, 1, 0)):
        for r in range(4):
            fz[r, 256 * i + 32 * r : 256 * i + 32 * r + SIDE, :] = qz[which]
    forward_z(ion)

    forward_y(e_ion, range(0, 4))
    taylor(1)
    forward_y(e_ion, range(4, 7))
    put_total(e_ion, ion_total)

    pl.semaphore_wait(ready_a, 3)
    for step in range(1, 4):
        pl.semaphore_signal(
            ready_b, inc=1, device_id=dev(s, (d + 8 * step) & (DOMAINS - 1)), device_id_type=MESH
        )

    taylor(2)
    build_x_tables()
    taylor(3)
    pl.semaphore_wait(ready_b, 3)

    def div(value, by):
        return lax.div(value, jnp.int32(by))

    def owner_dev(p):
        place_of = p + div(p * 7, 25)
        return dev((place_of & 1) * 2 + other, place_of >> 1)

    def sent_rows(p):
        tens = div(p, 10)
        return pl.ds(pl.multiple_of((4 * tens + 2 * p) * 8, 16), 16)

    def column_rows(p, half_of):
        return pl.ds(pl.multiple_of((2 * p + half_of) * 16, 16), 16)

    def wrap(value, count):
        return jnp.where(value >= count, value - count, value)

    ion_first = lax.rem(d, jnp.int32(25))
    rho_first = (chip * 25) >> 5

    def send_ion(j):
        p = 2 * wrap(j + ion_first, 25) + ylo
        return pltpu.make_async_remote_copy(
            e_ion.at[sent_rows(p), :],
            recv_ion.at[pl.ds(pl.multiple_of(d * 16, 16), 16), :],
            ion_send, ion_recv, device_id=owner_dev(p), device_id_type=MESH,
        )

    def send_rho(j):
        p = wrap(j + rho_first, PAIRS)
        return pltpu.make_async_remote_copy(
            e_rho.at[sent_rows(p), :],
            recv_rho.at[pl.ds(pl.multiple_of((ylo * DOMAINS + d) * 16, 16), 16), :],
            fwd_send, rho_recv, device_id=owner_dev(p), device_id_type=MESH,
        )

    def start_all(make, count):
        def one(j, carry):
            make(j).start()
            return carry

        lax.fori_loop(0, count, one, 0)

    start_all(send_ion, 25)

    rho_total = taylor(4)
    psi_copy = pltpu.make_async_copy(raw.at[pl.ds(0, 2800), :], psi_out, out_sem.at[0])
    psi_copy.start()

    forward_z(rho_cols)
    forward_y(e_rho, range(7))
    put_total(e_rho, rho_total)
    start_all(send_rho, PAIRS)

    half_rows = pl.ds(pl.multiple_of(core * 20, 4), 20)
    y_copy = pltpu.make_async_remote_copy(
        rho_chip.at[half_rows], rho_y, y_send, y_recv, device_id=across, device_id_type=MESH
    )
    y_copy.start()

    def await_bytes(ref, sem):
        pltpu.make_async_copy(ref, ref, sem).wait()

    def send_back(j):
        q = (j + chip) & (CHIPS - 1)
        return pltpu.make_async_remote_copy(
            result.at[pl.ds(pl.multiple_of((q >> 1) * 16, 16), 16), :],
            spec.at[pl.ds(pl.multiple_of((2 * pair_of + core) * 16, 16), 16), :],
            back_send, back_recv,
            device_id=dev((q & 1) * 2 + other, q >> 1), device_id_type=MESH,
        )

    @pl.when(is_owner)
    def _():
        await_bytes(recv_ion, ion_recv)
        await_bytes(recv_rho, rho_recv)
        ions = recv_ion[...].reshape(DOMAINS, 2, 8, 128)
        dens = recv_rho[...].reshape(2, DOMAINS, 2, 8, 128)
        dens = dens[0] + dens[1]
        sub8 = lax.broadcasted_iota(i32, (8, 128), 0)

        def total_of(array):
            rows = jnp.sum(array[:, 0], axis=0)
            return jnp.sum(jnp.where(sub8 == 7, rows, 0.0), axis=(0, 1), keepdims=True)

        scale = total_of(dens) / total_of(ions)
        charge = dens - scale.reshape(1, 1, 1, 1) * ions
        right = jnp.concatenate(
            [charge[:, 0].reshape(256, 128), charge[:, 1].reshape(256, 128)], axis=1
        )
        waves = dot(x_fwd[...], stack_right(right)) * coulomb[...]
        w_high, w_low = split(waves)
        back = dot(x_inv[0], w_high) + (dot(x_inv[0], w_low) + dot(x_inv[1], w_high))
        result[...] = jnp.stack(
            [back[:, 0:128].reshape(DOMAINS, 8, 128), back[:, 128:256].reshape(DOMAINS, 8, 128)],
            axis=1,
        ).reshape(DOMAINS * 16, 128)
        start_all(send_back, CHIPS)

    y_copy.wait_recv()

    def root(i, carry):
        value = (3.0 / math.pi) * (rho_chip[core * 20 + i] + rho_y[i])
        positive = value > 1.0e-37
        safe = jnp.where(positive, value, 1.0)
        guess = jnp.exp(jnp.log(safe) * (1.0 / 3.0))
        guess = (2.0 * guess + safe / (guess * guess)) * (1.0 / 3.0)
        xc[core * 20 + i] = jnp.where(positive, guess, 0.0)
        return carry

    lax.fori_loop(0, 20, root, 0)
    xc_copy = pltpu.make_async_remote_copy(
        xc.at[half_rows], xc.at[half_rows], xc_send, xc_recv,
        device_id=partner, device_id_type=MESH,
    )
    xc_copy.start()

    await_bytes(spec.at[pl.ds(0, 800), :], back_recv)

    def swap(p):
        rows = column_rows(p, other)
        return pltpu.make_async_remote_copy(
            spec.at[rows, :], spec.at[rows, :], mid_send, mid_recv,
            device_id=partner, device_id_type=MESH,
        )

    start_all(swap, PAIRS)
    await_bytes(spec.at[pl.ds(0, 800), :], mid_recv)

    for slot in range(7):
        rows = pl.ds(slot, SIDE, stride=8)
        main = spec[rows, :]
        tail = spec[pl.ds(SIDE * 8 + slot, 40, stride=8), :]
        parts = [tail] + [pltpu.roll(tail, 128 - 32 * j, 1) for j in range(1, 4)]
        right = jnp.concatenate([main, jnp.concatenate(parts, axis=0)], axis=1)
        out = dot(iy[...], stack_right(right))
        za[rows, :] = out[:, 0:128]
        zb[rows, :] = out[:, 128:256]
    carried = None
    for r in range(4):
        left = jnp.concatenate(
            [za[r * 320 : (r + 1) * 320, :], zb[r * 320 : (r + 1) * 320, :]], axis=1
        )
        high, low = split(left)
        out = dot_t(high, fz[r, 0:256, :] ) + dot_t(high, fz[r, 256:512, :])
        out = out + dot_t(low, fz[r, 0:256, :])
        piece = out[:, 0:128]
        if carried is not None:
            piece = piece + carried
        hsc[r] = piece
        carried = out[:, 128:256]
    hsc[4] = carried

    xc_copy.wait_recv()

    def finish(g, carry):
        for j in range(5):
            value = hsc[j, rows_of(g), :] - xc[g, :, 128 * j : 128 * j + 128]
            value = jnp.where(half[j, rows_of(g), :] > 0.0, value, 0.0)
            field[:, lanes_of(g, j)] = value[0:7, :]
        return carry

    lax.fori_loop(0, GROUPS, finish, 0)
    field_copy = pltpu.make_async_copy(field, field_out, out_sem.at[1])
    field_copy.start()

    for k in range(TERMS):
        def drain(ch, carry, k=k):
            to_low, to_high = edge_sends(k, ch)

            @pl.when(has_low)
            def _():
                to_low.wait_send()

            @pl.when(has_high)
            def _():
                to_high.wait_send()

            return carry

        lax.fori_loop(0, CHUNKS, drain, 0)

    def drain_rho(ch, carry):
        share_rho(ch).wait_send()
        return carry

    lax.fori_loop(0, CHUNKS, drain_rho, 0)
    y_copy.wait_send()
    xc_copy.wait_send()
    await_bytes(e_ion.at[pl.ds(0, 400), :], ion_send)
    await_bytes(e_rho.at[pl.ds(0, 800), :], fwd_send)
    await_bytes(spec.at[pl.ds(0, 800), :], mid_send)

    @pl.when(is_owner)
    def _():
        await_bytes(recv_rho, back_send)

    psi_copy.wait()
    field_copy.wait()


def step(orbitals, occupation, potential, background, layer_start):
    tabs = [jnp.asarray(t) for t in tables()]
    vmem = lambda *shape: pltpu.VMEM(shape, f32)
    dma = pltpu.SemaphoreType.DMA
    anyspace = pl.BlockSpec(memory_space=pl.ANY)
    smem = pl.BlockSpec(memory_space=pltpu.SMEM)
    edge = (TERMS, CHUNKS, 2, 5, CHUNK_GROUPS, 128)
    cube = (GROUPS, 8, LANES)
    columns = (1600, 128)
    tile5 = (5, 8 * GROUPS, 128)
    padded = (2, 5, 8 * GROUPS + 16, 128)
    scratch = [
        vmem(3000, 128), vmem(LAYERS, PLANE), vmem(LAYERS, PLANE),
        *[pltpu.VMEM(t.shape, bf16) for t in tabs],
        pltpu.VMEM((4, 768, 256), bf16),
        vmem(*padded), vmem(*padded), vmem(2, *tile5), vmem(*tile5), vmem(*tile5), vmem(*tile5),
        vmem(*edge), vmem(*edge), vmem(*edge), vmem(*edge),
        vmem(*cube), vmem(*cube), vmem(*cube), vmem(*tile5), vmem(20, 8, LANES), vmem(*cube),
        vmem(1280, 128), vmem(1280, 128), vmem(960, 128), vmem(960, 128),
        vmem(1024, 128), vmem(512, 128), vmem(512, 128), vmem(*columns),
        vmem(*tile5), vmem(LAYERS, PLANE),
        pltpu.VMEM((SIDE, 768), bf16), pltpu.VMEM((2, 256, SIDE), bf16), vmem(SIDE, 256),
        dma((3,)), dma((5,)), dma((2,)),
        dma((TERMS, CHUNKS)), dma((TERMS, CHUNKS)), dma((TERMS, CHUNKS)), dma((TERMS, CHUNKS)),
        dma((CHUNKS,)), dma((CHUNKS,)),
        *[dma(()) for _ in range(12)],
        pltpu.SemaphoreType.REGULAR, pltpu.SemaphoreType.REGULAR,
    ]
    psi, field = pl.pallas_call(
        kernel,
        out_shape=(
            jax.ShapeDtypeStruct((2800, 128), f32),
            jax.ShapeDtypeStruct((LAYERS, PLANE), f32),
        ),
        in_specs=[smem, smem] + [anyspace] * 8,
        out_specs=(anyspace, anyspace),
        scratch_shapes=scratch,
        compiler_params=pltpu.CompilerParams(
            collective_id=0, has_side_effects=True, vmem_limit_bytes=60 * 1024 * 1024
        ),
    )(
        layer_start, occupation, orbitals.reshape(2800, 128), potential, background, *tabs
    )
    return psi.reshape(2, 1, LAYERS, PLANE), field


def solution(mesh):
    return jax.shard_map(
        step,
        mesh=mesh,
        in_specs=(
            P(None, "state", "domain", None),
            P("state"),
            P("domain", None),
            P("domain", None),
            P(),
        ),
        out_specs=(P(None, "state", "domain", None), P("domain", None)),
        check_vma=False,
    )
```

time: 80.1 us -> 70.6 us (0.88)
  local copies, waits for them, and re-layouts: 8.75 us -> 3.52 us
  Pallas kernels: 69.9 us -> 65.6 us
    pallas_call x1, Pallas kernels: 69.9 us -> 65.6 us  [step(): pl.pallas_call(kernel, out_shape=(jax.ShapeDtypeStruct((2800, 128), f32),...]
    unnamed x5 -> x4, local copies, waits for them, and re-layouts: 7.07 us -> 3.52 us
    reshape x1 -> x0, local copies, waits for them, and re-layouts: 1.68 us -> none  [step(): orbitals.reshape(2, LAYERS, PLANE)]
where the time goes in v1:
time: 70.6 us; the launch traced here: 70.4 us
  Pallas kernels  65.6 us (93%)
  local copies, waits for them, and re-layouts  3.52 us (5%)
  between operations  1.29 us (2%)
    pallas_call x1, Pallas kernels, step(): pl.pallas_call(kernel, out_shape=(jax.ShapeDtypeStruct((2800, 128), f32),...  65.6 us
    unnamed x4, local copies, waits for them, and re-layouts  3.52 us

profile of v1, /device:TPU:1, one launch (start us, length us, event | category | flops | bytes accessed | tf_op | source)
XLA Modules:
  0.0 70.4 jit_solution(14990248596366525530)
XLA Ops:
  1.3 65.6 %shard_map.113 = (f32[2800,128]{1,0:T(8,128)}, f32[7,25600]{1,0:T(8,128)}) custom-call(s32[33]{0:T(128)} %starts.1, f32[1]{0:T(128)S(6)} %copy.16.occ, f32[2800,128]{1,0:T(8,128)} %bitcast.2, f32[7,25600]{1,0:T(8,128)} %pot_hbm.1, f32[7,25600]{1,0:T(8,128)} %bg_hbm.1, bf16[2,160,256]{2,1,0:T(8,128)(2,1)} %constant.10.clone.qz_hbm, ...), custom_call_target="tpu_custom_call" | custom-call | tf_op jit(solution)/shard_map/pallas_call | solution.py:752
  66.9 0.0 copy-start
  66.9 2.6 %copy.17 = f32[2,1,7,25600]{3,1,2,0:T(1,128)} copy(f32[2,1,7,25600]{3,1,2,0:T(1,128)} %bitcast.3) | data formatting | bytes 2867200
  69.5 0.0 copy-done
  69.5 0.9 %copy.18 = f32[7,25600]{1,0:T(8,128)} copy(f32[7,25600]{1,0:T(8,128)S(1)} %copy-done) | data formatting | bytes 1433600
Async XLA Ops:
  66.9 2.6 %copy-start = (f32[7,25600]{1,0:T(8,128)S(1)}, f32[7,25600]{1,0:T(8,128)}, u32[]{:S(2)}) copy-start(f32[7,25600]{1,0:T(8,128)} %get-tuple-element.13) | copy-start | bytes 2150404

commit v2 on v1

--- a/solution.py
+++ b/solution.py
@@ -16,8 +16,8 @@
 PLANE = SIDE * SIDE
 GROUPS = 40
 LANES = 640
-CHUNKS = 5
-CHUNK_GROUPS = 8
+CHUNKS = 10
+CHUNK_GROUPS = 4
 OWNERS = 100
 PAIRS = 50
 DOMAINS = 32
@@ -254,8 +254,8 @@
         for c in range(2):
             for j in range(5):
                 view = cur.at[c, j]
-                send_lo[k, ch, c, j] = view[pl.ds(base, 8, stride=8), :]
-                send_hi[k, ch, c, j] = view[pl.ds(base + top_row, 8, stride=8), :]
+                send_lo[k, ch, c, j] = view[pl.ds(base, CHUNK_GROUPS, stride=8), :]
+                send_hi[k, ch, c, j] = view[pl.ds(base + top_row, CHUNK_GROUPS, stride=8), :]
 
     @pl.when(jnp.logical_not(has_low))
     def _():
@@ -320,21 +320,36 @@
                 def tile(c, v):
                     return src[c, v % 5, rows_of(g0 + 1 + v // 5), :]
 
-                applied = []
+                def turned(own, amount, cache):
+                    def at(v):
+                        if v not in cache:
+                            cache[v] = pltpu.roll(own(v), amount, 1)
+                        return cache[v]
+
+                    return at
+
                 for c in range(2):
-                    own = {v: tile(c, v) for v in range(-2, count + 2)}
-                    right1 = {v: pltpu.roll(own[v], 1, 1) for v in range(-1, count)}
-                    left1 = {v: pltpu.roll(own[v], 127, 1) for v in range(0, count + 1)}
-                    right32 = {v: pltpu.roll(own[v], 32, 1) for v in range(-2, count - 0)}
-                    left32 = {v: pltpu.roll(own[v], 96, 1) for v in range(1, count + 2)}
-                    out = []
+                    tiles = {}
+
+                    def own(v, c=c, tiles=tiles):
+                        if v not in tiles:
+                            tiles[v] = tile(c, v)
+                        return tiles[v]
+
+                    right1, left1, right32, left32 = (
+                        turned(own, amount, {}) for amount in (1, 127, 32, 96)
+                    )
+                    to = 1 - c
+                    scale = -factor if to else factor
                     for v in range(count):
                         j, gi = v % 5, bi * span + v // 5
-                        near = jnp.where(first_lane, right1[v - 1], right1[v]) + jnp.where(
-                            last_lane, left1[v + 1], left1[v]
+                        g = g0 + v // 5
+                        rows = rows_of(g)
+                        near = jnp.where(first_lane, right1(v - 1), right1(v)) + jnp.where(
+                            last_lane, left1(v + 1), left1(v)
                         )
-                        far = jnp.where(low_lanes, right32[v - 2], right32[v - 1]) + jnp.where(
-                            high_lanes, left32[v + 2], left32[v + 1]
+                        far = jnp.where(low_lanes, right32(v - 2), right32(v - 1)) + jnp.where(
+                            high_lanes, left32(v + 2), left32(v + 1)
                         )
                         low = jnp.broadcast_to(
                             halo_lo[k - 1, ch, c, j, pl.ds(gi, 1), :], (8, 128)
@@ -342,31 +357,24 @@
                         high = jnp.broadcast_to(
                             halo_hi[k - 1, ch, c, j, pl.ds(gi, 1), :], (8, 128)
                         )
-                        stacked = pltpu.roll(jnp.where(is_spare, low, own[v]), 1, 0) + pltpu.roll(
-                            jnp.where(is_above, high, own[v]), 7, 0
-                        )
-                        rows = rows_of(g0 + v // 5)
-                        out.append(
-                            diag[j, rows, :] * own[v]
+                        stacked = pltpu.roll(
+                            jnp.where(is_spare, low, own(v)), 1, 0
+                        ) + pltpu.roll(jnp.where(is_above, high, own(v)), 7, 0)
+                        fresh = scale * (
+                            diag[j, rows, :] * own(v)
                             - half[j, rows, :] * ((near + far) + stacked)
                         )
-                    applied.append(out)
-                for v in range(count):
-                    j = v % 5
-                    g = g0 + v // 5
-                    rows = rows_of(g)
-                    fresh = (factor * applied[1][v], -factor * applied[0][v])
-                    squares = zero
-                    for c in range(2):
-                        value = psi[c, j, rows, :] + fresh[c]
+                        value = psi[to, j, rows, :] + fresh
                         if k < TERMS:
-                            dst[c, j, rows_of(g + 1), :] = fresh[c]
-                            psi[c, j, rows, :] = value
+                            dst[to, j, rows_of(g + 1), :] = fresh
+                            psi[to, j, rows, :] = value
                         else:
-                            raw[pl.ds(c * 1400 + 5 * g + j, 7, stride=200), :] = value[0:7, :]
-                            squares = squares + value * value
-                    if k == TERMS:
-                        rho_own[g, :, 128 * j : 128 * j + 128] = occ[0] * squares
+                            raw[pl.ds(to * 1400 + 5 * g + j, 7, stride=200), :] = value[0:7, :]
+                            cols = slice(128 * j, 128 * j + 128)
+                            square = occ[0] * (value * value)
+                            if c:
+                                square = rho_own[g, :, cols] + square
+                            rho_own[g, :, cols] = square
                 return inner
 
             lax.fori_loop(0, CHUNK_GROUPS // span, block, 0)
@@ -574,11 +582,13 @@
     put_total(e_rho, rho_total)
     start_all(send_rho, PAIRS)
 
-    half_rows = pl.ds(pl.multiple_of(core * 20, 4), 20)
-    y_copy = pltpu.make_async_remote_copy(
-        rho_chip.at[half_rows], rho_y, y_send, y_recv, device_id=across, device_id_type=MESH
-    )
-    y_copy.start()
+    def share_sum(part):
+        return pltpu.make_async_remote_copy(
+            rho_chip.at[pl.ds(core * 20 + 10 * part, 10)], rho_y.at[pl.ds(10 * part, 10)],
+            y_send.at[part], y_recv.at[part], device_id=across, device_id_type=MESH,
+        )
+
+    share_sum(0).start()
 
     def await_bytes(ref, sem):
         pltpu.make_async_copy(ref, ref, sem).wait()
@@ -619,7 +629,7 @@
         ).reshape(DOMAINS * 16, 128)
         start_all(send_back, CHIPS)
 
-    y_copy.wait_recv()
+    share_sum(1).start()
 
     def root(i, carry):
         value = (3.0 / math.pi) * (rho_chip[core * 20 + i] + rho_y[i])
@@ -630,23 +640,24 @@
         xc[core * 20 + i] = jnp.where(positive, guess, 0.0)
         return carry
 
-    lax.fori_loop(0, 20, root, 0)
-    xc_copy = pltpu.make_async_remote_copy(
-        xc.at[half_rows], xc.at[half_rows], xc_send, xc_recv,
-        device_id=partner, device_id_type=MESH,
+    def share_root(part):
+        rows = pl.ds(core * 20 + 10 * part, 10)
+        return pltpu.make_async_remote_copy(
+            xc.at[rows], xc.at[rows], xc_send.at[part], xc_recv.at[part],
+            device_id=partner, device_id_type=MESH,
+        )
+
+    share_sum(0).wait_recv()
+    lax.fori_loop(0, 10, root, 0)
+    share_root(0).start()
+
+    await_bytes(spec.at[pl.ds(0, 800), :], back_recv)
+
+    halves_of = spec.reshape(PAIRS, 32, 128).at[:, pl.ds(pl.multiple_of(other * 16, 16), 16), :]
+    swap = pltpu.make_async_remote_copy(
+        halves_of, halves_of, mid_send, mid_recv, device_id=partner, device_id_type=MESH
     )
-    xc_copy.start()
-
-    await_bytes(spec.at[pl.ds(0, 800), :], back_recv)
-
-    def swap(p):
-        rows = column_rows(p, other)
-        return pltpu.make_async_remote_copy(
-            spec.at[rows, :], spec.at[rows, :], mid_send, mid_recv,
-            device_id=partner, device_id_type=MESH,
-        )
-
-    start_all(swap, PAIRS)
+    swap.start()
     await_bytes(spec.at[pl.ds(0, 800), :], mid_recv)
 
     for slot in range(7):
@@ -658,6 +669,9 @@
         out = dot(iy[...], stack_right(right))
         za[rows, :] = out[:, 0:128]
         zb[rows, :] = out[:, 128:256]
+    share_sum(1).wait_recv()
+    lax.fori_loop(10, 20, root, 0)
+    share_root(1).start()
     carried = None
     for r in range(4):
         left = jnp.concatenate(
@@ -673,7 +687,8 @@
         carried = out[:, 128:256]
     hsc[4] = carried
 
-    xc_copy.wait_recv()
+    share_root(0).wait_recv()
+    share_root(1).wait_recv()
 
     def finish(g, carry):
         for j in range(5):
@@ -707,8 +722,9 @@
         return carry
 
     lax.fori_loop(0, CHUNKS, drain_rho, 0)
-    y_copy.wait_send()
-    xc_copy.wait_send()
+    for part in range(2):
+        share_sum(part).wait_send()
+        share_root(part).wait_send()
     await_bytes(e_ion.at[pl.ds(0, 400), :], ion_send)
     await_bytes(e_rho.at[pl.ds(0, 800), :], fwd_send)
     await_bytes(spec.at[pl.ds(0, 800), :], mid_send)
@@ -719,6 +735,25 @@
 
     psi_copy.wait()
     field_copy.wait()
+
+
+def hand_over(psi_in, field_in, psi_out, field_out, psi_buf, field_buf, sems):
+    moves = []
+    for i in range(4):
+        rows = pl.ds(704 * i, 704 if i < 3 else 688)
+        moves.append((psi_in.at[rows, :], psi_buf.at[rows, :], psi_out.at[rows, :]))
+    for i in range(2):
+        lanes = pl.ds(12800 * i, 12800)
+        moves.append((field_in.at[:, lanes], field_buf.at[:, lanes], field_out.at[:, lanes]))
+    reads = [pltpu.make_async_copy(a, b, sems.at[0, i]) for i, (a, b, _) in enumerate(moves)]
+    writes = [pltpu.make_async_copy(b, c, sems.at[1, i]) for i, (_, b, c) in enumerate(moves)]
+    for read in reads:
+        read.start()
+    for read, write in zip(reads, writes):
+        read.wait()
+        write.start()
+    for write in writes:
+        write.wait()
 
 
 def step(orbitals, occupation, potential, background, layer_start):
@@ -746,7 +781,8 @@
         dma((3,)), dma((5,)), dma((2,)),
         dma((TERMS, CHUNKS)), dma((TERMS, CHUNKS)), dma((TERMS, CHUNKS)), dma((TERMS, CHUNKS)),
         dma((CHUNKS,)), dma((CHUNKS,)),
-        *[dma(()) for _ in range(12)],
+        *[dma((2,)) for _ in range(4)],
+        *[dma(()) for _ in range(8)],
         pltpu.SemaphoreType.REGULAR, pltpu.SemaphoreType.REGULAR,
     ]
     psi, field = pl.pallas_call(
@@ -764,6 +800,17 @@
     )(
         layer_start, occupation, orbitals.reshape(2800, 128), potential, background, *tabs
     )
+    psi, field = pl.pallas_call(
+        hand_over,
+        out_shape=(
+            jax.ShapeDtypeStruct((2800, 128), f32),
+            jax.ShapeDtypeStruct((LAYERS, PLANE), f32),
+        ),
+        in_specs=[anyspace, anyspace],
+        out_specs=(anyspace, anyspace),
+        scratch_shapes=[vmem(2800, 128), vmem(LAYERS, PLANE), dma((2, 6))],
+        compiler_params=pltpu.CompilerParams(vmem_limit_bytes=60 * 1024 * 1024),
+    )(psi, field)
     return psi.reshape(2, 1, LAYERS, PLANE), field
 
 

time: 70.6 us -> 68.6 us (0.972)
  local copies, waits for them, and re-layouts: 3.52 us -> 0 us
  Pallas kernels: 65.6 us -> 67.1 us
    unnamed x4 -> x0, local copies, waits for them, and re-layouts: 3.52 us -> none
    pallas_call x0 -> x1, Pallas kernels: none -> 2.45 us  [step(): pl.pallas_call(hand_over, out_shape=(jax.ShapeDtypeStruct((2800, 128), f3...]
    pallas_call x1, Pallas kernels: 65.6 us -> 64.7 us  [step(): pl.pallas_call(kernel, out_shape=(jax.ShapeDtypeStruct((2800, 128), f32),...]
where the time goes in v2:
time: 68.6 us; the launch traced here: 68.4 us
  Pallas kernels  67.1 us (98%)
  between operations  1.28 us (2%)
    pallas_call x1, Pallas kernels, step(): pl.pallas_call(kernel, out_shape=(jax.ShapeDtypeStruct((2800, 128), f32),...  64.7 us
    pallas_call x1, Pallas kernels, step(): pl.pallas_call(hand_over, out_shape=(jax.ShapeDtypeStruct((2800, 128), f3...  2.45 us

profile of v2, /device:TPU:1, one launch (start us, length us, event | category | flops | bytes accessed | tf_op | source)
XLA Modules:
  0.0 68.4 jit_solution(10952790871297571316)
XLA Ops:
  1.3 64.7 %shard_map.113 = (f32[2800,128]{1,0:T(8,128)}, f32[7,25600]{1,0:T(8,128)}) custom-call(s32[33]{0:T(128)} %starts.1, f32[1]{0:T(128)S(6)} %copy.14.occ, f32[2800,128]{1,0:T(8,128)} %bitcast.2, f32[7,25600]{1,0:T(8,128)} %pot_hbm.1, f32[7,25600]{1,0:T(8,128)} %bg_hbm.1, bf16[2,160,256]{2,1,0:T(8,128)(2,1)} %constant.10.clone.qz_hbm, ...), custom_call_target="tpu_custom_call" | custom-call | tf_op jit(solution)/shard_map/pallas_call | solution.py:788
  66.0 2.4 %shard_map.114 = (f32[2800,128]{1,0:T(8,128)}, f32[7,25600]{1,0:T(8,128)}) custom-call(f32[2800,128]{1,0:T(8,128)} %get-tuple-element.6.psi_in, f32[7,25600]{1,0:T(8,128)} %get-tuple-element.7.field_in), custom_call_target="tpu_custom_call" | custom-call | tf_op jit(solution)/shard_map/pallas_call | solution.py:803

commit v3 on v2

--- a/solution.py
+++ b/solution.py
@@ -528,15 +528,12 @@
     taylor(3)
     pl.semaphore_wait(ready_b, 3)
 
-    def div(value, by):
-        return lax.div(value, jnp.int32(by))
-
     def owner_dev(p):
-        place_of = p + div(p * 7, 25)
+        place_of = p + ((p * (7 * 5243)) >> 17)
         return dev((place_of & 1) * 2 + other, place_of >> 1)
 
     def sent_rows(p):
-        tens = div(p, 10)
+        tens = (p * 205) >> 11
         return pl.ds(pl.multiple_of((4 * tens + 2 * p) * 8, 16), 16)
 
     def column_rows(p, half_of):
@@ -584,7 +581,8 @@
 
     def share_sum(part):
         return pltpu.make_async_remote_copy(
-            rho_chip.at[pl.ds(core * 20 + 10 * part, 10)], rho_y.at[pl.ds(10 * part, 10)],
+            rho_chip.at[pl.ds(core * 20 + 15 * part, 15 - 10 * part)],
+            rho_y.at[pl.ds(15 * part, 15 - 10 * part)],
             y_send.at[part], y_recv.at[part], device_id=across, device_id_type=MESH,
         )
 
@@ -641,14 +639,14 @@
         return carry
 
     def share_root(part):
-        rows = pl.ds(core * 20 + 10 * part, 10)
+        rows = pl.ds(core * 20 + 15 * part, 15 - 10 * part)
         return pltpu.make_async_remote_copy(
             xc.at[rows], xc.at[rows], xc_send.at[part], xc_recv.at[part],
             device_id=partner, device_id_type=MESH,
         )
 
     share_sum(0).wait_recv()
-    lax.fori_loop(0, 10, root, 0)
+    lax.fori_loop(0, 15, root, 0)
     share_root(0).start()
 
     await_bytes(spec.at[pl.ds(0, 800), :], back_recv)
@@ -658,6 +656,9 @@
         halves_of, halves_of, mid_send, mid_recv, device_id=partner, device_id_type=MESH
     )
     swap.start()
+    share_sum(1).wait_recv()
+    lax.fori_loop(15, 20, root, 0)
+    share_root(1).start()
     await_bytes(spec.at[pl.ds(0, 800), :], mid_recv)
 
     for slot in range(7):
@@ -669,9 +670,6 @@
         out = dot(iy[...], stack_right(right))
         za[rows, :] = out[:, 0:128]
         zb[rows, :] = out[:, 128:256]
-    share_sum(1).wait_recv()
-    lax.fori_loop(10, 20, root, 0)
-    share_root(1).start()
     carried = None
     for r in range(4):
         left = jnp.concatenate(
@@ -697,9 +695,14 @@
             field[:, lanes_of(g, j)] = value[0:7, :]
         return carry
 
-    lax.fori_loop(0, GROUPS, finish, 0)
-    field_copy = pltpu.make_async_copy(field, field_out, out_sem.at[1])
-    field_copy.start()
+    field_copies = []
+    for part in range(4):
+        lax.fori_loop(10 * part, 10 * part + 10, finish, 0)
+        lanes = pl.ds(6400 * part, 6400)
+        field_copies.append(
+            pltpu.make_async_copy(field.at[:, lanes], field_out.at[:, lanes], out_sem.at[1 + part])
+        )
+        field_copies[-1].start()
 
     for k in range(TERMS):
         def drain(ch, carry, k=k):
@@ -734,7 +737,8 @@
         await_bytes(recv_rho, back_send)
 
     psi_copy.wait()
-    field_copy.wait()
+    for copy in field_copies:
+        copy.wait()
 
 
 def hand_over(psi_in, field_in, psi_out, field_out, psi_buf, field_buf, sems):
@@ -778,7 +782,7 @@
         vmem(1024, 128), vmem(512, 128), vmem(512, 128), vmem(*columns),
         vmem(*tile5), vmem(LAYERS, PLANE),
         pltpu.VMEM((SIDE, 768), bf16), pltpu.VMEM((2, 256, SIDE), bf16), vmem(SIDE, 256),
-        dma((3,)), dma((5,)), dma((2,)),
+        dma((3,)), dma((5,)), dma((5,)),
         dma((TERMS, CHUNKS)), dma((TERMS, CHUNKS)), dma((TERMS, CHUNKS)), dma((TERMS, CHUNKS)),
         dma((CHUNKS,)), dma((CHUNKS,)),
         *[dma((2,)) for _ in range(4)],

time: 68.6 us -> 67 us (0.977)
  Pallas kernels: 67.1 us -> 65.5 us
    pallas_call x1, Pallas kernels: 64.7 us -> 63.1 us  [step(): pl.pallas_call(kernel, out_shape=(jax.ShapeDtypeStruct((2800, 128), f32),...]
where the time goes in v3:
time: 67 us; the launch traced here: 66.8 us
  Pallas kernels  65.5 us (98%)
  between operations  1.28 us (2%)
    pallas_call x1, Pallas kernels, step(): pl.pallas_call(kernel, out_shape=(jax.ShapeDtypeStruct((2800, 128), f32),...  63.1 us
    pallas_call x1, Pallas kernels, step(): pl.pallas_call(hand_over, out_shape=(jax.ShapeDtypeStruct((2800, 128), f3...  2.45 us

profile of v3, /device:TPU:1, one launch (start us, length us, event | category | flops | bytes accessed | tf_op | source)
XLA Modules:
  0.0 66.8 jit_solution(15515915252856463610)
XLA Ops:
  1.3 63.1 %shard_map.113 = (f32[2800,128]{1,0:T(8,128)}, f32[7,25600]{1,0:T(8,128)}) custom-call(s32[33]{0:T(128)} %starts.1, f32[1]{0:T(128)S(6)} %copy.14.occ, f32[2800,128]{1,0:T(8,128)} %bitcast.2, f32[7,25600]{1,0:T(8,128)} %pot_hbm.1, f32[7,25600]{1,0:T(8,128)} %bg_hbm.1, bf16[2,160,256]{2,1,0:T(8,128)(2,1)} %constant.10.clone.qz_hbm, ...), custom_call_target="tpu_custom_call" | custom-call | tf_op jit(solution)/shard_map/pallas_call | solution.py:792
  64.4 2.4 %shard_map.114 = (f32[2800,128]{1,0:T(8,128)}, f32[7,25600]{1,0:T(8,128)}) custom-call(f32[2800,128]{1,0:T(8,128)} %get-tuple-element.6.psi_in, f32[7,25600]{1,0:T(8,128)} %get-tuple-element.7.field_in), custom_call_target="tpu_custom_call" | custom-call | tf_op jit(solution)/shard_map/pallas_call | solution.py:807

commit v4 on v3

--- a/solution.py
+++ b/solution.py
@@ -16,8 +16,8 @@
 PLANE = SIDE * SIDE
 GROUPS = 40
 LANES = 640
-CHUNKS = 10
-CHUNK_GROUPS = 4
+CHUNKS = 5
+CHUNK_GROUPS = 8
 OWNERS = 100
 PAIRS = 50
 DOMAINS = 32

time: 67 us -> 66.9 us (level)
  no operation moved by 1% of the time
where the time goes in v4:
time: 66.9 us; the launch traced here: 66.7 us
  Pallas kernels  65.4 us (98%)
  between operations  1.28 us (2%)
    pallas_call x1, Pallas kernels, step(): pl.pallas_call(kernel, out_shape=(jax.ShapeDtypeStruct((2800, 128), f32),...  63 us
    pallas_call x1, Pallas kernels, step(): pl.pallas_call(hand_over, out_shape=(jax.ShapeDtypeStruct((2800, 128), f3...  2.45 us

profile of v4, /device:TPU:1, one launch (start us, length us, event | category | flops | bytes accessed | tf_op | source)
XLA Modules:
  0.0 66.7 jit_solution(13680934456039673437)
XLA Ops:
  1.3 63.0 %shard_map.113 = (f32[2800,128]{1,0:T(8,128)}, f32[7,25600]{1,0:T(8,128)}) custom-call(s32[33]{0:T(128)} %starts.1, f32[1]{0:T(128)S(6)} %copy.14.occ, f32[2800,128]{1,0:T(8,128)} %bitcast.2, f32[7,25600]{1,0:T(8,128)} %pot_hbm.1, f32[7,25600]{1,0:T(8,128)} %bg_hbm.1, bf16[2,160,256]{2,1,0:T(8,128)(2,1)} %constant.10.clone.qz_hbm, ...), custom_call_target="tpu_custom_call" | custom-call | tf_op jit(solution)/shard_map/pallas_call | solution.py:792
  64.3 2.4 %shard_map.114 = (f32[2800,128]{1,0:T(8,128)}, f32[7,25600]{1,0:T(8,128)}) custom-call(f32[2800,128]{1,0:T(8,128)} %get-tuple-element.6.psi_in, f32[7,25600]{1,0:T(8,128)} %get-tuple-element.7.field_in), custom_call_target="tpu_custom_call" | custom-call | tf_op jit(solution)/shard_map/pallas_call | solution.py:807
